TPU v7x, 32 devices: a whole 2x2x4 slice. The times are simulated.
32 devices in a mesh: blk: 2 (over core), head: 16 (over z, y, x).
Axes of the slice: x: 2, y: 2, z: 4, core: 2. Of those that a mesh axis runs over, the one named last changes fastest.
Arguments:
- tokens_qkv: bfloat16 [2048, 12288], P(('blk', 'head')), may hold values from -8 to 8, as said below
- block_mask: int32 [16, 16], replicated, may hold values from 0 to 1, as said below
Outputs:
- attended: bfloat16 [2048, 4096], P(('blk', 'head'))
Inputs may be any that keep to these rules, and one draw needn't show every extreme that they name: `tokens_qkv`: queries, keys and values ordered by head, then query, key, value, then the 128 entries. `block_mask`: 1 where a pair of 128-token blocks attends; a block always attends to itself whatever the entry says.
All inputs are finite; a program needn't handle non-finite values.
Results may differ from a plain program's by a relative error of at most 0.007.
Values may be sent and summed in bfloat16 or wider, within the bound.
No kernel may reach another device: no remote copies, remote signals or barrier semaphores. Data moves between devices by JAX's collectives and lax.ppermute only.
A program may use at most 64 MiB of HBM per device.

v0:
```python
import jax
import jax.numpy as jnp
from jax import lax
from jax.sharding import PartitionSpec as P

HD = 128
BLOCK = 128
NEGATIVE = -1e30


def shortened(x):

    def short(part):
        return part.astype(jnp.bfloat16) if part.dtype == jnp.float32 else part

    return jax.tree.map(short, x)


def shifted(x, axis, by):
    size = lax.axis_size(axis)
    return lax.ppermute(x, axis, [(i, (i + by) % size) for i in range(size)])


def live_pairs(block_mask, row_start, row_count, col_start, col_count):
    picked = lax.dynamic_slice(
        block_mask,
        (row_start // BLOCK, col_start // BLOCK),
        (row_count // BLOCK, col_count // BLOCK),
    )
    spread = jnp.broadcast_to(
        (picked == 1)[:, None, :, None], (row_count // BLOCK, BLOCK, col_count // BLOCK, BLOCK)
    ).reshape(row_count, col_count)
    row_blocks = (row_start + jnp.arange(row_count, dtype=jnp.int32)) // BLOCK
    col_blocks = (col_start + jnp.arange(col_count, dtype=jnp.int32)) // BLOCK
    return spread | (row_blocks[:, None] == col_blocks[None, :])


def attend(running, queries, keys_part, values_part, live_map):
    outputs, maxima, totals = running
    key_count = keys_part.shape[0]
    stride = min(key_count, 512)
    factor_scale = queries.shape[-1] ** (-0.5)
    for offset in range(0, key_count, stride):
        scores = (
            jnp.einsum(
                "qhd,khd->qhk",
                queries,
                keys_part[offset : offset + stride],
                preferred_element_type=jnp.float32,
            )
            * factor_scale
        )
        allowed = live_map[:, None, offset : offset + stride]
        scores = jnp.where(allowed, scores, NEGATIVE)
        newest = jnp.maximum(maxima, jnp.max(scores, axis=-1))
        weights = jnp.where(allowed, jnp.exp(scores - newest[..., None]), 0.0)
        factor = jnp.exp(maxima - newest)
        totals = totals * factor + jnp.sum(weights, axis=-1)
        outputs = outputs * factor[..., None] + jnp.einsum(
            "qhk,khd->qhd",
            weights.astype(jnp.bfloat16),
            values_part[offset : offset + stride],
            preferred_element_type=jnp.float32,
        )
        maxima = newest
    return (outputs, maxima, totals)


def empty_state(row_total, head_count):
    return (
        jnp.zeros((row_total, head_count, HD), jnp.float32),
        jnp.full((row_total, head_count), NEGATIVE, jnp.float32),
        jnp.zeros((row_total, head_count), jnp.float32),
    )


def on_device(tokens_qkv, block_mask):
    by_heads = lax.all_to_all(tokens_qkv, "head", split_axis=1, concat_axis=0, tiled=True)
    rows_here = by_heads.shape[0]
    head_count = by_heads.shape[1] // (3 * HD)
    packed = by_heads.reshape(rows_here, head_count, 3, HD)
    queries = packed[:, :, 0]
    keys_here = packed[:, :, 1]
    values_here = packed[:, :, 2]
    cycle_size = lax.axis_size("blk")
    own_index = lax.axis_index("blk")
    half_rows = rows_here // 2
    own_start = own_index * rows_here
    running = attend(
        empty_state(rows_here, head_count),
        queries,
        keys_here,
        values_here,
        live_pairs(block_mask, own_start, rows_here, own_start, rows_here),
    )

    def advance(hop_index, cycle_state):
        upward = shifted(shortened(cycle_state[1]), "blk", 1)
        downward = shifted(shortened(cycle_state[2]), "blk", -1)
        forward = (own_index - hop_index) % cycle_size
        backward = (own_index + hop_index) % cycle_size
        updated = attend(
            cycle_state[0],
            queries,
            upward[0],
            upward[1],
            live_pairs(block_mask, own_start, rows_here, forward * rows_here, half_rows),
        )
        updated = attend(
            updated,
            queries,
            downward[0],
            downward[1],
            live_pairs(
                block_mask, own_start, rows_here, backward * rows_here + half_rows, half_rows
            ),
        )
        return (updated, upward, downward)

    start_up = (keys_here[:half_rows], values_here[:half_rows])
    start_down = (keys_here[half_rows:], values_here[half_rows:])
    running, unused_up, unused_down = lax.fori_loop(
        1, cycle_size, advance, (running, start_up, start_down)
    )
    outputs, totals = (running[0], running[2])
    result = (outputs / totals[..., None]).astype(jnp.bfloat16).reshape(rows_here, head_count * HD)
    return lax.all_to_all(result, "head", split_axis=0, concat_axis=1, tiled=True)


def solution(mesh):
    return jax.shard_map(
        on_device,
        mesh=mesh,
        in_specs=(P(("blk", "head"), None), P()),
        out_specs=P(("blk", "head"), None),
        check_vma=False,
    )
```

profile of v0, /device:TPU:0, one launch (start us, length us, event | category | flops | bytes accessed | tf_op | source)
XLA Modules:
  0.0 96.2 jit_solution(4603364310684311930)
XLA Ops:
  0.0 2.7 %copy.66 = bf16[8,16,8,768]{3,2,0,1:T(8,128)(2,1)} copy(bf16[8,16,8,768]{3,2,1,0:T(8,128)(2,1)} %bitcast.149) | data formatting | bytes 3145728 | tf_op jit(solution)/shard_map/all_to_all | solution.py:78
  2.7 8.3 %all-to-all-start = ((bf16[64,16,768]{2,0,1:T(8,128)(2,1)}), bf16[64,16,768]{2,0,1:T(8,128)(2,1)S(1)}, u32[]{:S(2)}, u32[]{:S(2)}) async-start(bf16[64,16,768]{2,0,1:T(8,128)(2,1)} %bitcast.139), calls=%async_computation | async-start | bytes 3145728 | tf_op jit(solution)/shard_map/all_to_all | solution.py:78
  12.0 0.9 bitcast_or_fusion
  13.0 1.1 %fusion.84 = (pred[1024,512]{0,1:T(8,128)(4,1)}, pred[1024,512]{0,1:T(8,128)(4,1)}) fusion(pred[1024,1024]{0,1:T(8,128)(4,1)S(1)} %bitcast_or_fusion), kind=kLoop, calls=%fused_computation.100 | loop fusion | bytes 2097152 | tf_op jit(solution)/shard_map/slice | solution.py:53
  14.4 1.0 bitcast_or_fusion.2
  15.4 29.8 %all-to-all-done = bf16[64,16,768]{2,0,1:T(8,128)(2,1)S(1)} async-done(((bf16[64,16,768]{2,0,1:T(8,128)(2,1)}), bf16[64,16,768]{2,0,1:T(8,128)(2,1)S(1)}, u32[]{:S(2)}, u32[]{:S(2)}) %all-to-all-start) | async-done | bytes 1572896 | tf_op jit(solution)/shard_map/all_to_all | solution.py:78
  45.2 1.2 %copy-done = bf16[64,16,768]{2,0,1:T(8,128)(2,1)} copy-done((bf16[64,16,768]{2,0,1:T(8,128)(2,1)}, bf16[64,16,768]{2,0,1:T(8,128)(2,1)S(1)}, u32[]{:S(2)}) %copy-start) | copy-done | bytes 1572888
  46.3 4.2 %reshape.241 = bf16[1024,2,3,128]{3,2,1,0:T(4,128)(2,1)S(1)} reshape(bf16[16,64,768]{2,1,0:T(8,128)(2,1)} %bitcast.144) | data formatting | bytes 3145728 | tf_op jit(solution)/shard_map/reshape | solution.py:81
  50.5 0.7 slice.56
  51.3 1.9 %fusion.83 = (bf16[512,2,1,128]{3,2,1,0:T(2,128)(2,1)S(1)}, bf16[512,2,1,128]{3,2,1,0:T(2,128)(2,1)S(1)}, bf16[512,2,1,128]{3,2,1,0:T(2,128)(2,1)S(1)}, bf16[512,2,1,128]{3,2,1,0:T(2,128)(2,1)S(1)}) fusion(bf16[1024,2,3,128]{3,2,1,0:T(4,128)(2,1)S(1)} %reshape.241), kind=kLoop, calls=%fused_computation.99 | loop fusion | bytes 2097152 | tf_op jit(solution)/shard_map/slice | solution.py:62
  53.5 0.5 collective-permute-start
  54.5 1.0 %fusion = (f32[1024,2]{0,1:T(2,128)S(1)}, f32[2,512,1024]{2,1,0:T(8,128)S(1)}) fusion(pred[1024,512]{0,1:T(8,128)(4,1)S(1)} %copy-done.2, bf16[512,2,128]{2,0,1:T(8,128)(2,1)S(1)} %bitcast.155, bf16[1024,2,1,128]{3,2,1,0:T(2,128)(2,1)S(1)} %slice.56), kind=kOutput, calls=%fused_computation.9 | convolution fusion | flops 271579136 | bytes 5513216 | tf_op jit(solution)/shard_map/qhd,khd->qhk/dot_general | solution.py:45
  55.6 1.0 %fusion.1 = (f32[1024,2]{0,1:T(2,128)S(1)}, f32[2,512,1024]{2,1,0:T(8,128)S(1)}) fusion(pred[1024,512]{0,1:T(8,128)(4,1)S(1)} %copy-done.1, bf16[512,2,128]{2,0,1:T(8,128)(2,1)S(1)} %bitcast.157, bf16[1024,2,1,128]{3,2,1,0:T(2,128)(2,1)S(1)} %slice.56), kind=kOutput, calls=%fused_computation.10 | convolution fusion | flops 271579136 | bytes 5513216 | tf_op jit(solution)/shard_map/qhd,khd->qhk/dot_general | solution.py:45
  56.6 1.0 %fusion.3 = (f32[1024,2]{0,1:T(2,128)S(1)}, f32[2,512,1024]{2,1,0:T(8,128)S(1)}) fusion(pred[1024,512]{0,1:T(8,128)(4,1)S(1)} %get-tuple-element.62, bf16[512,2,128]{2,0,1:T(8,128)(2,1)S(1)} %collective-permute-done.2, bf16[1024,2,1,128]{3,2,1,0:T(2,128)(2,1)S(1)} %slice.56), kind=kOutput, calls=%fused_computation.12 | convolution fusion | flops 271579136 | bytes 5513216 | tf_op jit(solution)/shard_map/while/body/eval_jaxpr/qhd,khd->qhk/dot_general | solution.py:45
  57.6 1.0 %fusion.2 = (f32[1024,2]{0,1:T(2,128)S(1)}, f32[2,512,1024]{2,1,0:T(8,128)S(1)}) fusion(pred[1024,512]{0,1:T(8,128)(4,1)S(1)} %get-tuple-element.61, bf16[512,2,128]{2,0,1:T(8,128)(2,1)S(1)} %collective-permute-done, bf16[1024,2,1,128]{3,2,1,0:T(2,128)(2,1)S(1)} %slice.56), kind=kOutput, calls=%fused_computation.11 | convolution fusion | flops 271579136 | bytes 5513216 | tf_op jit(solution)/shard_map/while/body/eval_jaxpr/qhd,khd->qhk/dot_general | solution.py:45
  58.7 2.3 %fusion.4 = (f32[1024,2]{0,1:T(2,128)S(1)}, f32[1024,2]{0,1:T(2,128)S(1)}) fusion(f32[2,512,1024]{2,1,0:T(8,128)S(1)} %get-tuple-element.70, f32[1024,2]{0,1:T(2,128)S(1)} %get-tuple-element.58, pred[1024,512]{0,1:T(8,128)(4,1)S(1)} %copy-done.2, f32[1024,2]{0,1:T(2,128)S(1)} %get-tuple-element.35, f32[2,512,1024]{2,1,0:T(8,128)S(1)} %get-tuple-element.68, ...), kind=kLoop, calls=%fused_computation.13 | loop fusion | flops 10481664 | bytes 9469952 | tf_op jit(solution)/shard_map/reduce_sum | solution.py:58
  61.0 2.4 %fusion.8 = (f32[1024,2]{0,1:T(2,128)S(1)}, f32[1024,2]{0,1:T(2,128)S(1)}) fusion(f32[2,512,1024]{2,1,0:T(8,128)S(1)} %get-tuple-element.66, f32[1024,2]{0,1:T(2,128)S(1)} %get-tuple-element.34, pred[1024,512]{0,1:T(8,128)(4,1)S(1)} %get-tuple-element.61, f32[1024,2]{0,1:T(2,128)S(1)} %get-tuple-element.33, f32[2,512,1024]{2,1,0:T(8,128)S(1)} %get-tuple-element.64, ...), kind=kLoop, calls=%fused_computation.17 | loop fusion | flops 10481664 | bytes 9469952 | tf_op jit(solution)/shard_map/while/body/eval_jaxpr/reduce_sum | solution.py:58
  63.5 2.3 %fusion.45 = f32[1024,2,128]{2,0,1:T(8,128)S(1)} fusion(bf16[512,2,128]{2,0,1:T(8,128)(2,1)S(1)} %bitcast.151, f32[2,512,1024]{2,1,0:T(8,128)S(1)} %get-tuple-element.70, f32[1024,2]{0,1:T(2,128)S(1)} %get-tuple-element.58, pred[1024,512]{0,1:T(8,128)(4,1)S(1)} %copy-done.2, f32[1024,2]{0,1:T(2,128)S(1)} %get-tuple-element.32, ...), kind=kOutput, calls=%fused_computation.39 | convolution fusion | flops 274202624 | bytes 6053888 | tf_op jit(solution)/shard_map/qhk,khd->qhd/dot_general | solution.py:59
  65.8 2.0 %fusion.48 = f32[1024,2,128]{2,0,1:T(8,128)S(1)} fusion(f32[1024,2,128]{2,0,1:T(8,128)S(1)} %fusion.45, bf16[512,2,128]{2,0,1:T(8,128)(2,1)S(1)} %bitcast.153, f32[2,512,1024]{2,1,0:T(8,128)S(1)} %get-tuple-element.68, f32[1024,2]{0,1:T(2,128)S(1)} %get-tuple-element.35, pred[1024,512]{0,1:T(8,128)(4,1)S(1)} %copy-done.1, f32[1024,2]{0,1:T(2,128)S(1)} %get-tuple-element.31), kind=kOutput, calls=%fused_computation.40 | convolution fusion | flops 274202624 | bytes 7094272 | tf_op jit(solution)/shard_map/qhk,khd->qhd/dot_general | solution.py:59
  67.8 1.7 %fusion.33 = f32[1024,2,128]{2,0,1:T(8,128)S(1)} fusion(bf16[512,2,128]{2,0,1:T(8,128)(2,1)S(1)} %collective-permute-done.3, f32[2,512,1024]{2,1,0:T(8,128)S(1)} %get-tuple-element.64, f32[1024,2]{0,1:T(2,128)S(1)} %get-tuple-element.33, pred[1024,512]{0,1:T(8,128)(4,1)S(1)} %get-tuple-element.62), kind=kOutput, calls=%fused_computation.35 | convolution fusion | flops 273678336 | bytes 6037504 | tf_op jit(solution)/shard_map/while/body/eval_jaxpr/qhk,khd->qhd/dot_general | solution.py:59
  69.5 2.2 %divide_convert_fusion = bf16[1024,2,128]{2,0,1:T(8,128)(2,1)S(1)} fusion(f32[1024,2,128]{2,0,1:T(8,128)S(1)} %fusion.33, f32[1024,2,128]{2,0,1:T(8,128)S(1)} %fusion.48, bf16[512,2,128]{2,0,1:T(8,128)(2,1)S(1)} %collective-permute-done.1, f32[2,512,1024]{2,1,0:T(8,128)S(1)} %get-tuple-element.66, f32[1024,2]{0,1:T(2,128)S(1)} %get-tuple-element.34, ...), kind=kOutput, calls=%fused_computation.43 | convolution fusion | flops 274989056 | bytes 7626752 | tf_op jit(solution)/shard_map/while/body/eval_jaxpr/qhk,khd->qhd/dot_general | solution.py:59
  71.7 0.5 copy.37
  72.5 22.9 %all_to_all.35 = bf16[16,64,256]{2,1,0:T(8,128)(2,1)S(1)} all-to-all(bf16[16,64,256]{2,1,0:T(8,128)(2,1)S(1)} %all_to_all.29), channel_id=1, replica_groups=mesh['blk'=2,'head'=16] {'head'}, dimensions={0} | all-to-all | bytes 1048576 | tf_op jit(solution)/shard_map/all_to_all | solution.py:127
  95.4 0.8 copy.49
  (32 shorter events, 2.4 us)
Async XLA Ops:
  0.0 11.2 %copy-start.3 = (s32[16,16]{1,0:T(8,128)S(1)}, s32[16,16]{1,0:T(8,128)}, u32[]{:S(2)}) copy-start(s32[16,16]{1,0:T(8,128)} %param.3) | copy-start | bytes 3076
  2.7 42.4 %all-to-all-start = ((bf16[64,16,768]{2,0,1:T(8,128)(2,1)}), bf16[64,16,768]{2,0,1:T(8,128)(2,1)S(1)}, u32[]{:S(2)}, u32[]{:S(2)}) async-start(bf16[64,16,768]{2,0,1:T(8,128)(2,1)} %bitcast.139), calls=%async_computation | async-start | bytes 3145728 | tf_op jit(solution)/shard_map/all_to_all | solution.py:78
  45.2 1.2 %copy-start = (bf16[64,16,768]{2,0,1:T(8,128)(2,1)}, bf16[64,16,768]{2,0,1:T(8,128)(2,1)S(1)}, u32[]{:S(2)}) copy-start(bf16[64,16,768]{2,0,1:T(8,128)(2,1)S(1)} %all-to-all-done) | copy-start | bytes 4718596
  51.2 3.3 %copy-start.2 = (pred[1024,512]{0,1:T(8,128)(4,1)S(1)}, pred[1024,512]{0,1:T(8,128)(4,1)}, u32[]{:S(2)}) copy-start(pred[1024,512]{0,1:T(8,128)(4,1)} %get-tuple-element.54) | copy-start | bytes 1572868
  53.3 2.3 %copy-start.1 = (pred[1024,512]{0,1:T(8,128)(4,1)S(1)}, pred[1024,512]{0,1:T(8,128)(4,1)}, u32[]{:S(2)}) copy-start(pred[1024,512]{0,1:T(8,128)(4,1)} %get-tuple-element.56) | copy-start | bytes 1572868
  53.4 14.4 %collective-permute-start.3 = (bf16[512,2,128]{2,0,1:T(8,128)(2,1)S(1)}, bf16[512,2,128]{2,0,1:T(8,128)(2,1)S(1)}, u32[]{:S(2)}, u32[]{:S(2)}) collective-permute-start(bf16[512,2,128]{2,0,1:T(8,128)(2,1)S(1)} %bitcast.152), channel_id=1, source_target_pairs={{0,16},{16,0},{1,17},{17,1},{2,18},{18,2},{3,19},{19,3},{4,20},{20... | collective-permute-start | bytes 786440 | tf_op jit(solution)/shard_map/while/body/eval_jaxpr/ppermute | solution.py:21
  53.5 4.1 %collective-permute-start = (bf16[512,2,128]{2,0,1:T(8,128)(2,1)S(1)}, bf16[512,2,128]{2,0,1:T(8,128)(2,1)S(1)}, u32[]{:S(2)}, u32[]{:S(2)}) collective-permute-start(bf16[512,2,128]{2,0,1:T(8,128)(2,1)S(1)} %bitcast.154), channel_id=1, source_target_pairs={{0,16},{16,0},{1,17},{17,1},{2,18},{18,2},{3,19},{19,3},{4,20},{20... | collective-permute-start | bytes 786440 | tf_op jit(solution)/shard_map/while/body/eval_jaxpr/ppermute | solution.py:21
  54.0 2.6 %collective-permute-start.2 = (bf16[512,2,128]{2,0,1:T(8,128)(2,1)S(1)}, bf16[512,2,128]{2,0,1:T(8,128)(2,1)S(1)}, u32[]{:S(2)}, u32[]{:S(2)}) collective-permute-start(bf16[512,2,128]{2,0,1:T(8,128)(2,1)S(1)} %bitcast.156), channel_id=1, source_target_pairs={{0,16},{16,0},{1,17},{17,1},{2,18},{18,2},{3,19},{19,3},{4,20},{20... | collective-permute-start | bytes 786440 | tf_op jit(solution)/shard_map/while/body/eval_jaxpr/ppermute | solution.py:21
  54.1 15.4 %collective-permute-start.1 = (bf16[512,2,128]{2,0,1:T(8,128)(2,1)S(1)}, bf16[512,2,128]{2,0,1:T(8,128)(2,1)S(1)}, u32[]{:S(2)}, u32[]{:S(2)}) collective-permute-start(bf16[512,2,128]{2,0,1:T(8,128)(2,1)S(1)} %bitcast.150), channel_id=1, source_target_pairs={{0,16},{16,0},{1,17},{17,1},{2,18},{18,2},{3,19},{19,3},{4,20},{20... | collective-permute-start | bytes 786440 | tf_op jit(solution)/shard_map/while/body/eval_jaxpr/ppermute | solution.py:21
where the time goes:
time: 96.5 us; the launch traced here: 96.2 us
  waiting for transfers between devices  29.8 us (31%)
  blocking collectives  22.9 us (24%)
  local copies, waits for them, and re-layouts  14.7 us (15%)
  matrix products  12.2 us (13%)
  starting transfers between devices  9.42 us (10%)
  other arithmetic  6.84 us (7%)
    all_to_all x1, waiting for transfers between devices, on_device(): lax.all_to_all(tokens_qkv, 'head', split_axis=1, concat_axis=0, tiled=True)  29.8 us
    all_to_all x1, blocking collectives, on_device(): lax.all_to_all(result, 'head', split_axis=0, concat_axis=1, tiled=True)  22.9 us
    all_to_all x1, starting transfers between devices, on_device(): lax.all_to_all(tokens_qkv, 'head', split_axis=1, concat_axis=0, tiled=True)  8.34 us
    dot_general x4, matrix products, attend(): jnp.einsum('qhk,khd->qhd', weights.astype(jnp.bfloat16), values_part[offs...  8.14 us
    reduce_sum x2, other arithmetic, attend(): totals = totals * factor + jnp.sum(weights, axis=-1)  4.69 us
    reshape x1, local copies, waits for them, and re-layouts, on_device(): packed = by_heads.reshape(rows_here, head_count, 3, HD)  4.16 us
    dot_general x4, matrix products, attend(): jnp.einsum('qhd,khd->qhk', queries, keys_part[offset:offset + stride], pr...  4.1 us
    all_to_all x1, local copies, waits for them, and re-layouts, on_device(): lax.all_to_all(tokens_qkv, 'head', split_axis=1, concat_axis=0, tiled=True)  2.74 us
  transfers between devices with their start and end apart: 5, of which 1 were waited for; matrix products, arithmetic and copies ran while one was open for 20% of the time, Pallas kernels for 0%

commit v1 on v0

--- a/solution.py
+++ b/solution.py
@@ -6,6 +6,9 @@
 HD = 128
 BLOCK = 128
 NEGATIVE = -1e30
+time_sheet = lambda a0: jnp.concatenate(
+    lax.all_to_all(jnp.stack(jnp.split(a0, lax.psum(1, "head"), 1), 0), "head", 0, 0), 0
+)
 
 
 def shortened(x):
@@ -75,7 +78,7 @@
 
 
 def on_device(tokens_qkv, block_mask):
-    by_heads = lax.all_to_all(tokens_qkv, "head", split_axis=1, concat_axis=0, tiled=True)
+    by_heads = time_sheet(tokens_qkv)
     rows_here = by_heads.shape[0]
     head_count = by_heads.shape[1] // (3 * HD)
     packed = by_heads.reshape(rows_here, head_count, 3, HD)

time: 96.5 us -> 124 us (1.28)
  local copies, waits for them, and re-layouts: 14.7 us -> 41.8 us
    unnamed x12 -> x27, local copies, waits for them, and re-layouts: 1.36 us -> 27.8 us
    another operation x0 -> x2, local copies, waits for them, and re-layouts: none -> 5.69 us  [the longest x1 4.16 us: on_device(): packed = by_heads.reshape(rows_here, head_count, 3, HD)]
    reshape x1 -> x0, local copies, waits for them, and re-layouts: 4.16 us -> none  [on_device(): packed = by_heads.reshape(rows_here, head_count, 3, HD)]
    all_to_all x1 -> x0, local copies, waits for them, and re-layouts: 2.74 us -> none  [on_device(): lax.all_to_all(tokens_qkv, 'head', split_axis=1, concat_axis=0, tiled=True)]
    dot_general x4, matrix products: 8.14 us -> 6.44 us  [attend(): jnp.einsum('qhk,khd->qhd', weights.astype(jnp.bfloat16), values_part[offs...]
    dot_general x4, matrix products: 4.1 us -> 5.44 us  [attend(): jnp.einsum('qhd,khd->qhk', queries, keys_part[offset:offset + stride], pr...]
  transfers between devices with their start and end apart: 5 -> 5, of which waited for: 1 -> 1; matrix products, arithmetic and copies ran while one was open for 20% -> 16% of each run, Pallas kernels for 0% -> 0%
where the time goes in v1:
time: 124 us; the launch traced here: 123 us
  local copies, waits for them, and re-layouts  41.8 us (34%)
  waiting for transfers between devices  29.9 us (24%)
  blocking collectives  22.9 us (18%)
  matrix products  11.9 us (10%)
  starting transfers between devices  9.46 us (8%)
  other arithmetic  6.82 us (6%)
    all_to_all x1, waiting for transfers between devices, lax.all_to_all(jnp.stack(jnp.split(a0, lax.psum(1, 'head'), 1), 0), 'head...  29.9 us
    unnamed x27, local copies, waits for them, and re-layouts  27.8 us
    all_to_all x1, blocking collectives, on_device(): lax.all_to_all(result, 'head', split_axis=0, concat_axis=1, tiled=True)  22.9 us
    all_to_all x1, starting transfers between devices, lax.all_to_all(jnp.stack(jnp.split(a0, lax.psum(1, 'head'), 1), 0), 'head...  8.39 us
    dot_general x4, matrix products, attend(): jnp.einsum('qhk,khd->qhd', weights.astype(jnp.bfloat16), values_part[offs...  6.44 us
    dot_general x4, matrix products, attend(): jnp.einsum('qhd,khd->qhk', queries, keys_part[offset:offset + stride], pr...  5.44 us
    reduce_sum x2, other arithmetic, attend(): totals = totals * factor + jnp.sum(weights, axis=-1)  4.7 us
    another operation x1, local copies, waits for them, and re-layouts, on_device(): packed = by_heads.reshape(rows_here, head_count, 3, HD)  4.16 us
  transfers between devices with their start and end apart: 5, of which 1 were waited for; matrix products, arithmetic and copies ran while one was open for 16% of the time, Pallas kernels for 0%

profile of v1, /device:TPU:0, one launch (start us, length us, event | category | flops | bytes accessed | tf_op | source)
XLA Modules:
  0.0 123.1 jit_solution(18393822409372000905)
XLA Ops:
  0.0 1.5 %bitcast_dynamic-update-slice_fusion.15 = bf16[16,64,768]{2,1,0:T(8,128)(2,1)} fusion(bf16[64,12288]{1,0:T(8,128)(2,1)} %param.2), kind=kLoop, calls=%fused_computation.61 | loop fusion | bytes 196608
  1.5 1.5 %bitcast_dynamic-update-slice_fusion.14 = bf16[16,64,768]{2,1,0:T(8,128)(2,1)} fusion(bf16[16,64,768]{2,1,0:T(8,128)(2,1)} %bitcast_dynamic-update-slice_fusion.15, bf16[64,12288]{1,0:T(8,128)(2,1)} %param.2), kind=kLoop, calls=%fused_computation.60 | loop fusion | bytes 196608
  3.1 1.5 %bitcast_dynamic-update-slice_fusion.13 = bf16[16,64,768]{2,1,0:T(8,128)(2,1)} fusion(bf16[16,64,768]{2,1,0:T(8,128)(2,1)} %bitcast_dynamic-update-slice_fusion.14, bf16[64,12288]{1,0:T(8,128)(2,1)} %param.2), kind=kLoop, calls=%fused_computation.59 | loop fusion | bytes 196608
  6.1 1.5 %bitcast_dynamic-update-slice_fusion.11 = bf16[16,64,768]{2,1,0:T(8,128)(2,1)} fusion(bf16[16,64,768]{2,1,0:T(8,128)(2,1)} %bitcast_dynamic-update-slice_fusion.12, bf16[64,12288]{1,0:T(8,128)(2,1)} %param.2), kind=kLoop, calls=%fused_computation.57 | loop fusion | bytes 196608
  7.7 1.5 %bitcast_dynamic-update-slice_fusion.10 = bf16[16,64,768]{2,1,0:T(8,128)(2,1)} fusion(bf16[16,64,768]{2,1,0:T(8,128)(2,1)} %bitcast_dynamic-update-slice_fusion.11, bf16[64,12288]{1,0:T(8,128)(2,1)} %param.2), kind=kLoop, calls=%fused_computation.56 | loop fusion | bytes 196608
  9.2 1.5 %bitcast_dynamic-update-slice_fusion.9 = bf16[16,64,768]{2,1,0:T(8,128)(2,1)} fusion(bf16[16,64,768]{2,1,0:T(8,128)(2,1)} %bitcast_dynamic-update-slice_fusion.10, bf16[64,12288]{1,0:T(8,128)(2,1)} %param.2), kind=kLoop, calls=%fused_computation.55 | loop fusion | bytes 196608
  10.7 1.5 %bitcast_dynamic-update-slice_fusion.8 = bf16[16,64,768]{2,1,0:T(8,128)(2,1)} fusion(bf16[16,64,768]{2,1,0:T(8,128)(2,1)} %bitcast_dynamic-update-slice_fusion.9, bf16[64,12288]{1,0:T(8,128)(2,1)} %param.2), kind=kLoop, calls=%fused_computation.54 | loop fusion | bytes 196608
  12.3 1.5 %bitcast_dynamic-update-slice_fusion.7 = bf16[16,64,768]{2,1,0:T(8,128)(2,1)} fusion(bf16[16,64,768]{2,1,0:T(8,128)(2,1)} %bitcast_dynamic-update-slice_fusion.8, bf16[64,12288]{1,0:T(8,128)(2,1)} %param.2), kind=kLoop, calls=%fused_computation.53 | loop fusion | bytes 196608
  15.3 1.5 %bitcast_dynamic-update-slice_fusion.5 = bf16[16,64,768]{2,1,0:T(8,128)(2,1)} fusion(bf16[16,64,768]{2,1,0:T(8,128)(2,1)} %bitcast_dynamic-update-slice_fusion.6, bf16[64,12288]{1,0:T(8,128)(2,1)} %param.2), kind=kLoop, calls=%fused_computation.51 | loop fusion | bytes 196608
  18.4 1.5 %bitcast_dynamic-update-slice_fusion.3 = bf16[16,64,768]{2,1,0:T(8,128)(2,1)} fusion(bf16[16,64,768]{2,1,0:T(8,128)(2,1)} %bitcast_dynamic-update-slice_fusion.4, bf16[64,12288]{1,0:T(8,128)(2,1)} %param.2), kind=kLoop, calls=%fused_computation.49 | loop fusion | bytes 196608
  21.4 1.5 %bitcast_dynamic-update-slice_fusion.1 = bf16[16,64,768]{2,1,0:T(8,128)(2,1)} fusion(bf16[16,64,768]{2,1,0:T(8,128)(2,1)} %bitcast_dynamic-update-slice_fusion.2, bf16[64,12288]{1,0:T(8,128)(2,1)} %param.2), kind=kLoop, calls=%fused_computation.47 | loop fusion | bytes 196608
  23.0 1.5 %bitcast_dynamic-update-slice_fusion = bf16[16,64,768]{2,1,0:T(8,128)(2,1)} fusion(bf16[16,64,768]{2,1,0:T(8,128)(2,1)} %bitcast_dynamic-update-slice_fusion.1, bf16[64,12288]{1,0:T(8,128)(2,1)} %param.2), kind=kLoop, calls=%fused_computation.46 | loop fusion | bytes 196608 | tf_op jit(solution)/shard_map/stack | solution.py:10
  24.5 8.4 %all-to-all-start = ((bf16[16,64,768]{2,1,0:T(8,128)(2,1)}), bf16[16,64,768]{2,1,0:T(8,128)(2,1)}, u32[]{:S(2)}, u32[]{:S(2)}) async-start(bf16[16,64,768]{2,1,0:T(8,128)(2,1)} %bitcast_dynamic-update-slice_fusion), calls=%async_computation | async-start | bytes 3145728 | tf_op jit(solution)/shard_map/all_to_all | solution.py:10
  37.2 29.9 %all-to-all-done = bf16[16,64,768]{2,1,0:T(8,128)(2,1)} async-done(((bf16[16,64,768]{2,1,0:T(8,128)(2,1)}), bf16[16,64,768]{2,1,0:T(8,128)(2,1)}, u32[]{:S(2)}, u32[]{:S(2)}) %all-to-all-start) | async-done | bytes 1572896 | tf_op jit(solution)/shard_map/all_to_all | solution.py:10
  67.1 4.2 %reshape_reshape.3 = bf16[1024,2,3,128]{3,2,1,0:T(4,128)(2,1)S(1)} reshape(bf16[16,64,768]{2,1,0:T(8,128)(2,1)} %all-to-all-done) | data formatting | bytes 3145728 | tf_op jit(solution)/shard_map/reshape;reshape | solution.py:84
  71.2 1.7 %slice.56 = bf16[1024,2,1,128]{3,2,1,0:T(2,128)(2,1)} slice(bf16[1024,2,3,128]{3,2,1,0:T(4,128)(2,1)S(1)} %reshape_reshape.3), slice={[0:1024], [0:2], [0:1], [0:128]} | slice | bytes 1048576 | tf_op jit(solution)/shard_map/slice | solution.py:85
  72.9 3.0 %fusion.85 = (bf16[512,2,1,128]{3,2,1,0:T(2,128)(2,1)}, bf16[512,2,1,128]{3,2,1,0:T(2,128)(2,1)}, bf16[512,2,1,128]{3,2,1,0:T(2,128)(2,1)}, bf16[512,2,1,128]{3,2,1,0:T(2,128)(2,1)}) fusion(bf16[1024,2,3,128]{3,2,1,0:T(4,128)(2,1)S(1)} %reshape_reshape.3), kind=kLoop, calls=%fused_computation.114 | loop fusion | bytes 2097152 | tf_op jit(solution)/shard_map/slice | solution.py:65
  81.8 2.4 %fusion.1 = (f32[1024,2]{0,1:T(2,128)S(1)}, f32[2,512,1024]{2,1,0:T(8,128)S(1)}) fusion(pred[1024,512]{0,1:T(8,128)(4,1)} %get-tuple-element.56, bf16[512,2,128]{2,0,1:T(8,128)(2,1)S(1)} %bitcast.176, bf16[1024,2,1,128]{3,2,1,0:T(2,128)(2,1)} %slice.56), kind=kOutput, calls=%fused_computation.10 | convolution fusion | flops 271579136 | bytes 5513216 | tf_op jit(solution)/shard_map/qhd,khd->qhk/dot_general | solution.py:48
  87.4 2.3 %fusion.4 = (f32[1024,2]{0,1:T(2,128)S(1)}, f32[1024,2]{0,1:T(2,128)S(1)}) fusion(f32[2,512,1024]{2,1,0:T(8,128)S(1)} %get-tuple-element.70, f32[1024,2]{0,1:T(2,128)S(1)} %get-tuple-element.58, pred[1024,512]{0,1:T(8,128)(4,1)S(1)} %copy-done.1, f32[1024,2]{0,1:T(2,128)S(1)} %get-tuple-element.35, f32[2,512,1024]{2,1,0:T(8,128)S(1)} %get-tuple-element.68, ...), kind=kLoop, calls=%fused_computation.13 | loop fusion | flops 10481664 | bytes 9469952 | tf_op jit(solution)/shard_map/reduce_sum | solution.py:61
  89.6 2.4 %fusion.8 = (f32[1024,2]{0,1:T(2,128)S(1)}, f32[1024,2]{0,1:T(2,128)S(1)}) fusion(f32[2,512,1024]{2,1,0:T(8,128)S(1)} %get-tuple-element.66, f32[1024,2]{0,1:T(2,128)S(1)} %get-tuple-element.34, pred[1024,512]{0,1:T(8,128)(4,1)S(1)} %get-tuple-element.61, f32[1024,2]{0,1:T(2,128)S(1)} %get-tuple-element.33, f32[2,512,1024]{2,1,0:T(8,128)S(1)} %get-tuple-element.64, ...), kind=kLoop, calls=%fused_computation.17 | loop fusion | flops 10481664 | bytes 9469952 | tf_op jit(solution)/shard_map/while/body/eval_jaxpr/reduce_sum | solution.py:61
  92.1 1.7 %fusion.54 = f32[1024,2,128]{0,2,1:T(8,128)S(1)} fusion(f32[2,512,1024]{2,1,0:T(8,128)S(1)} %get-tuple-element.70, f32[1024,2]{0,1:T(2,128)S(1)} %get-tuple-element.58, pred[1024,512]{0,1:T(8,128)(4,1)S(1)} %copy-done.1, f32[1024,2]{0,1:T(2,128)S(1)} %get-tuple-element.32, f32[1024,2]{0,1:T(2,128)S(1)} %get-tuple-element.57, ...), kind=kOutput, calls=%fused_computation.41 | convolution fusion | flops 274202624 | bytes 6053888 | tf_op jit(solution)/shard_map/qhk,khd->qhd/dot_general | solution.py:62
  93.8 1.7 %fusion.48 = f32[1024,2,128]{0,2,1:T(8,128)S(1)} fusion(f32[1024,2,128]{0,2,1:T(8,128)S(1)} %fusion.54, f32[2,512,1024]{2,1,0:T(8,128)S(1)} %get-tuple-element.68, f32[1024,2]{0,1:T(2,128)S(1)} %get-tuple-element.35, pred[1024,512]{0,1:T(8,128)(4,1)S(1)} %copy-done, f32[1024,2]{0,1:T(2,128)S(1)} %get-tuple-element.31, bf16[512,2,1,128]{0,3,1,2:T(8,128)(2,1)S(1)} %copy.50), kind=kOutput, calls=%fused_computation.39 | convolution fusion | flops 274202624 | bytes 7094272 | tf_op jit(solution)/shard_map/qhk,khd->qhd/dot_general | solution.py:62
  97.0 1.6 %divide_convert_fusion = bf16[1024,2,128]{0,2,1:T(8,128)(2,1)S(1)} fusion(f32[1024,2,128]{0,2,1:T(8,128)S(1)} %fusion.33, f32[1024,2,128]{0,2,1:T(8,128)S(1)} %fusion.48, bf16[512,2,128]{0,2,1:T(8,128)(2,1)S(1)} %collective-permute-done.1, f32[2,512,1024]{2,1,0:T(8,128)S(1)} %get-tuple-element.66, f32[1024,2]{0,1:T(2,128)S(1)} %get-tuple-element.34, ...), kind=kOutput, calls=%fused_computation.42 | convolution fusion | flops 274989056 | bytes 7626752 | tf_op jit(solution)/shard_map/while/body/eval_jaxpr/qhk,khd->qhd/dot_general | solution.py:62
  99.4 22.9 %all_to_all.24 = bf16[16,64,256]{2,1,0:T(8,128)(2,1)S(1)} all-to-all(bf16[16,64,256]{2,1,0:T(8,128)(2,1)S(1)} %all_to_all.18), channel_id=1, replica_groups=mesh['blk'=2,'head'=16] {'head'}, dimensions={0} | all-to-all | bytes 1048576 | tf_op jit(solution)/shard_map/all_to_all | solution.py:130
  (47 shorter events, 22.3 us)
Async XLA Ops:
  0.0 33.0 %copy-start.3 = (s32[16,16]{1,0:T(8,128)S(1)}, s32[16,16]{1,0:T(8,128)}, u32[]{:S(2)}) copy-start(s32[16,16]{1,0:T(8,128)} %param.3) | copy-start | bytes 3076
  24.5 42.6 %all-to-all-start = ((bf16[16,64,768]{2,1,0:T(8,128)(2,1)}), bf16[16,64,768]{2,1,0:T(8,128)(2,1)}, u32[]{:S(2)}, u32[]{:S(2)}) async-start(bf16[16,64,768]{2,1,0:T(8,128)(2,1)} %bitcast_dynamic-update-slice_fusion), calls=%async_computation | async-start | bytes 3145728 | tf_op jit(solution)/shard_map/all_to_all | solution.py:10
  77.2 7.1 %copy-start.1 = (pred[1024,512]{0,1:T(8,128)(4,1)S(1)}, pred[1024,512]{0,1:T(8,128)(4,1)}, u32[]{:S(2)}) copy-start(pred[1024,512]{0,1:T(8,128)(4,1)} %get-tuple-element.54) | copy-start | bytes 1572868
  77.2 7.1 %copy-start.2 = (bf16[1024,2,1,128]{3,2,1,0:T(2,128)(2,1)S(1)}, bf16[1024,2,1,128]{3,2,1,0:T(2,128)(2,1)}, u32[]{:S(2)}) copy-start(bf16[1024,2,1,128]{3,2,1,0:T(2,128)(2,1)} %slice.56) | copy-start | bytes 1572868
  80.7 5.6 %collective-permute-start.2 = (bf16[512,2,128]{2,0,1:T(8,128)(2,1)S(1)}, bf16[512,2,128]{2,0,1:T(8,128)(2,1)S(1)}, u32[]{:S(2)}, u32[]{:S(2)}) collective-permute-start(bf16[512,2,128]{2,0,1:T(8,128)(2,1)S(1)} %bitcast.175), channel_id=1, source_target_pairs={{0,16},{16,0},{1,17},{17,1},{2,18},{18,2},{3,19},{19,3},{4,20},{20... | collective-permute-start | bytes 786440 | tf_op jit(solution)/shard_map/while/body/eval_jaxpr/ppermute | solution.py:24
  80.8 4.5 %collective-permute-start = (bf16[512,2,128]{2,0,1:T(8,128)(2,1)S(1)}, bf16[512,2,128]{2,0,1:T(8,128)(2,1)S(1)}, u32[]{:S(2)}, u32[]{:S(2)}) collective-permute-start(bf16[512,2,128]{2,0,1:T(8,128)(2,1)S(1)} %bitcast.177), channel_id=1, source_target_pairs={{0,16},{16,0},{1,17},{17,1},{2,18},{18,2},{3,19},{19,3},{4,20},{20... | collective-permute-start | bytes 786440 | tf_op jit(solution)/shard_map/while/body/eval_jaxpr/ppermute | solution.py:24
  81.3 14.2 %collective-permute-start.3 = (bf16[512,2,128]{0,2,1:T(8,128)(2,1)S(1)}, bf16[512,2,128]{0,2,1:T(8,128)(2,1)S(1)}, u32[]{:S(2)}, u32[]{:S(2)}) collective-permute-start(bf16[512,2,128]{0,2,1:T(8,128)(2,1)S(1)} %bitcast.174), channel_id=1, source_target_pairs={{0,16},{16,0},{1,17},{17,1},{2,18},{18,2},{3,19},{19,3},{4,20},{20... | collective-permute-start | bytes 786440 | tf_op jit(solution)/shard_map/while/body/eval_jaxpr/ppermute | solution.py:24
  81.4 15.6 %collective-permute-start.1 = (bf16[512,2,128]{0,2,1:T(8,128)(2,1)S(1)}, bf16[512,2,128]{0,2,1:T(8,128)(2,1)S(1)}, u32[]{:S(2)}, u32[]{:S(2)}) collective-permute-start(bf16[512,2,128]{0,2,1:T(8,128)(2,1)S(1)} %bitcast.173), channel_id=1, source_target_pairs={{0,16},{16,0},{1,17},{17,1},{2,18},{18,2},{3,19},{19,3},{4,20},{20... | collective-permute-start | bytes 786440 | tf_op jit(solution)/shard_map/while/body/eval_jaxpr/ppermute | solution.py:24
  86.3 1.1 copy-start
